TPU v7x, 512 devices: a whole 4x4x16 slice. The times are simulated.
512 devices in a mesh: dp: 32 (over y, x, core), mp: 16 (over z).
Axes of the slice: x: 4, y: 4, z: 16, core: 2. Of those that a mesh axis runs over, the one named last changes fastest.
Arguments:
- tokens: bfloat16 [32768, 8192], P('dp', 'mp'), may hold values from -6 to 6
- value_weight: bfloat16 [8192, 1024], P('mp'), may hold values from -0.0625 to 0.0625
- down_panels: bfloat16 [256, 8192, 64], P('dp', 'mp'), may hold values from -0.0625 to 0.0625
- up_panels: bfloat16 [256, 64, 1024], P('dp'), may hold values from -0.75 to 0.75
- cotangent: bfloat16 [32768, 1024], P(('dp', 'mp')), may hold values from -6 to 6
- block_adapter: int32 [256], replicated, may hold values from 0 to 255, as said below
- adapter_slot: int32 [256], replicated, may hold values from 0 to 255, as said below
Outputs:
- projected: bfloat16 [32768, 1024], P(('dp', 'mp'))
- grad_tokens: bfloat16 [32768, 8192], P('dp', 'mp')
- grad_down: bfloat16 [256, 8192, 64], P('dp', 'mp')
- grad_up: bfloat16 [256, 64, 1024], P('dp')
Inputs may be any that keep to these rules, and one draw needn't show every extreme that they name: `block_adapter`: the 8 blocks of one index of dp name adapters stored on 8 different owners, the owner of slot s being s // 8. `adapter_slot`: A permutation of the adapters.
All inputs are finite; a program needn't handle non-finite values.
Results may differ from a plain program's by a relative error of at most 0.005.
Values may be sent and summed in bfloat16 or wider, within the bound.
A program may use at most 128 MiB of HBM per device.

v0:
```python
import jax
import jax.numpy as jnp
from jax import lax
from jax.sharding import PartitionSpec as P

RANK = 64
BLOCK_ROWS = 128


def per_device(
    tokens, value_weight, down_panels, up_panels, cotangent, block_adapter, adapter_slot
):
    n_owners = lax.axis_size("dp")
    myself = lax.axis_index("dp")
    n_split = lax.axis_size("mp")
    my_part = lax.axis_index("mp")
    rows, width_dev = tokens.shape
    own_rows, kv_full = cotangent.shape
    kv_part = kv_full // n_split
    stored = down_panels.shape[0]
    blocks = rows // BLOCK_ROWS
    group = min(own_rows, BLOCK_ROWS)
    groups = own_rows // group
    highest = lax.Precision.HIGHEST
    hits = block_adapter[:, None] == jnp.arange(adapter_slot.shape[0], dtype=jnp.int32)[None, :]
    slots_all = jnp.sum(jnp.where(hits, adapter_slot[None, :], 0), axis=1)
    owner_all = (slots_all // stored).reshape(n_owners, blocks)
    local_all = (slots_all % stored).reshape(n_owners, blocks)
    mine = owner_all == myself
    wanted = jnp.sum(jnp.where(mine, local_all, 0), axis=1)
    served = jnp.any(mine, axis=1)
    pick_mask = (wanted[:, None] == jnp.arange(stored, dtype=jnp.int32)[None, :]) & served[:, None]
    pick_bf = pick_mask.astype(jnp.bfloat16)
    my_owner = lax.dynamic_index_in_dim(owner_all, myself, 0, keepdims=False)
    select_mask = my_owner[:, None] == jnp.arange(n_owners, dtype=jnp.int32)[None, :]
    select_bf = select_mask.astype(jnp.bfloat16)
    select_f32 = select_mask.astype(jnp.float32)
    send_a = jnp.einsum(
        "ra,adk->rdk", pick_bf, down_panels, preferred_element_type=jnp.float32
    ).astype(jnp.bfloat16)
    send_b = jnp.einsum(
        "ra,akc->rkc", pick_bf, up_panels, preferred_element_type=jnp.float32
    ).astype(jnp.bfloat16)
    got_a, got_b = (
        lax.all_to_all(send_a, "dp", split_axis=0, concat_axis=0, tiled=True),
        lax.all_to_all(send_b, "dp", split_axis=0, concat_axis=0, tiled=True),
    )
    panel_a = jnp.einsum(
        "bo,odk->bdk", select_bf, got_a, preferred_element_type=jnp.float32
    ).astype(jnp.bfloat16)
    panel_b = jnp.einsum(
        "bo,okc->bkc", select_bf, got_b, preferred_element_type=jnp.float32
    ).astype(jnp.bfloat16)
    token_blocks = tokens.reshape(blocks, BLOCK_ROWS, width_dev)
    partial_value = jnp.dot(tokens, value_weight, preferred_element_type=jnp.float32)
    base = lax.psum_scatter(partial_value, "mp", scatter_dimension=0, tiled=True)
    down_part = jnp.einsum(
        "bnd,bdk->bnk", token_blocks, panel_a, preferred_element_type=jnp.float32
    )
    down = lax.psum(down_part, "mp").astype(jnp.bfloat16)
    first_row = my_part * own_rows
    my_down = lax.dynamic_slice_in_dim(down.reshape(rows, RANK), first_row, own_rows, 0).reshape(
        groups, group, RANK
    )
    group_blocks = (first_row + jnp.arange(groups, dtype=jnp.int32) * group) // BLOCK_ROWS
    my_up = jnp.take(panel_b, group_blocks, axis=0)
    lifted = jnp.einsum("gnk,gkc->gnc", my_down, my_up, preferred_element_type=jnp.float32)
    projected = (base + lifted.reshape(own_rows, kv_full)).astype(jnp.bfloat16)
    cot_all = lax.all_gather(cotangent, "mp", axis=0, tiled=True)
    grad_base = jnp.einsum("nc,dc->nd", cot_all, value_weight, preferred_element_type=jnp.float32)
    cot_blocks = cot_all.reshape(blocks, BLOCK_ROWS, kv_full)
    back = jnp.einsum(
        "bnc,bkc->bnk", cot_blocks, panel_b, preferred_element_type=jnp.float32
    ).astype(jnp.bfloat16)
    through = jnp.einsum("bnk,bdk->bnd", back, panel_a, preferred_element_type=jnp.float32)
    grad_tokens = (grad_base + through.reshape(rows, width_dev)).astype(jnp.bfloat16)
    block_grad_a = jnp.einsum(
        "bnd,bnk->bdk", token_blocks, back, preferred_element_type=jnp.float32
    )
    cot_share = lax.dynamic_slice_in_dim(cot_blocks, my_part * kv_part, kv_part, 2)
    block_grad_b = jnp.einsum("bnk,bnc->bkc", down, cot_share, preferred_element_type=jnp.float32)
    send_ga = jnp.einsum("bo,bdk->odk", select_f32, block_grad_a, precision=highest)
    send_gb = jnp.einsum("bo,bkc->okc", select_f32, block_grad_b, precision=highest)
    recv_ga, recv_gb = (
        lax.all_to_all(send_ga, "dp", split_axis=0, concat_axis=0, tiled=True),
        lax.all_to_all(send_gb, "dp", split_axis=0, concat_axis=0, tiled=True),
    )
    pick_f32 = pick_mask.astype(jnp.float32)
    grad_down = jnp.einsum("ra,rdk->adk", pick_f32, recv_ga, precision=highest).astype(jnp.bfloat16)
    grad_share = jnp.einsum("ra,rkc->akc", pick_f32, recv_gb, precision=highest).astype(
        jnp.bfloat16
    )
    grad_up = lax.all_gather(grad_share, "mp", axis=2, tiled=True)
    return (projected, grad_tokens, grad_down, grad_up)


def solution(mesh):
    placed = (
        P("dp", "mp"),
        P("mp", None),
        P("dp", "mp", None),
        P("dp", None, None),
        P(("dp", "mp"), None),
        P(),
        P(),
    )
    return jax.shard_map(
        per_device,
        mesh=mesh,
        in_specs=placed,
        out_specs=(P(("dp", "mp"), None), P("dp", "mp"), P("dp", "mp", None), P("dp", None, None)),
        check_vma=False,
    )
```

profile of v0, /device:TPU:2, one launch (start us, length us, event | category | flops | bytes accessed | tf_op | source)
XLA Modules:
  0.0 294.6 jit_solution(1035140061272832880)
XLA Ops:
  7.2 0.0 all-gather.3.cloned.1.call-start
  7.2 0.7 all-gather.3.cloned.1.call-update
  7.9 0.9 select_reduce_fusion
  8.8 0.1 reduce_sum.21
  8.9 0.1 fusion.56
  9.0 0.1 fusion.34
  9.1 1.8 convolution_convert_fusion.1
  11.0 2.5 copy.43
  13.5 9.6 %all-to-all-start = ((bf16[32,512,64]{1,2,0:T(8,128)(2,1)}), bf16[32,512,64]{1,2,0:T(8,128)(2,1)S(1)}, u32[]{:S(2)}, u32[]{:S(2)}) async-start(bf16[32,512,64]{1,2,0:T(8,128)(2,1)} %copy.43), calls=%async_computation.1 | async-start | bytes 4194304 | tf_op jit(solution)/shard_map/all_to_all | solution.py:45
  23.1 0.0 all-gather.5.cloned.1.call-start
  23.1 27.9 %all-to-all-done = bf16[32,512,64]{1,2,0:T(8,128)(2,1)S(1)} async-done(((bf16[32,512,64]{1,2,0:T(8,128)(2,1)}), bf16[32,512,64]{1,2,0:T(8,128)(2,1)S(1)}, u32[]{:S(2)}, u32[]{:S(2)}) %all-to-all-start) | async-done | bytes 2097184 | tf_op jit(solution)/shard_map/all_to_all | solution.py:45
  51.0 1.2 fusion.10
  52.3 0.8 copy-done.1
  53.1 0.5 convolution_bitcast_fusion.1
  53.5 63.4 %all-reduce.1 = bf16[8,128,64]{1,2,0:T(8,128)(2,1)S(1)} all-reduce(f32[8,128,64]{1,2,0:T(8,128)S(1)} %convolution_bitcast_fusion.1), channel_id=1, replica_groups=mesh['dp'=32,'mp'=16] {'mp'}, use_global_device_ids=true, to_apply=%region_4.5 | all-reduce | flops 65536 | bytes 393216 | tf_op jit(solution)/shard_map/psum | solution.py:60
  117.0 1.2 fusion.28
  118.2 0.7 fusion.26
  118.9 0.6 copy.57
  119.5 0.7 reshape.88
  120.2 14.8 %all_to_all.20 = f32[32,1,4096]{2,1,0:T(1,128)S(1)} all-to-all(f32[32,1,4096]{2,1,0:T(1,128)S(1)} %reshape.88), channel_id=1, replica_groups=mesh['dp'=32,'mp'=16] {'dp'}, dimensions={0} | all-to-all | bytes 1048576 | tf_op jit(solution)/shard_map/all_to_all | solution.py:86
  135.0 0.5 broadcast.68
  135.5 1.9 reduce
  137.4 0.4 reshape.89
  137.8 1.0 convolution_convert_fusion.2
  138.8 0.8 copy.59
  139.7 1.3 convolution_convert_fusion
  141.0 4.3 %copy.48 = bf16[32,64,1024]{2,1,0:T(8,128)(2,1)} copy(bf16[32,64,1024]{2,0,1:T(8,128)(2,1)S(1)} %convolution_convert_fusion) | data formatting | bytes 8388608 | tf_op jit(solution)/shard_map/convert_element_type | solution.py:43
  145.3 6.1 %all-to-all-start.1 = ((bf16[32,64,1024]{2,1,0:T(8,128)(2,1)}), bf16[32,64,1024]{2,1,0:T(8,128)(2,1)}, u32[]{:S(2)}, u32[]{:S(2)}) async-start(bf16[32,64,1024]{2,1,0:T(8,128)(2,1)} %copy.48), calls=%async_computation.2 | async-start | bytes 8388608 | tf_op jit(solution)/shard_map/all_to_all | solution.py:46
  151.4 0.3 reduce-scatter.2.cloned.1.call-start
  151.7 3.2 %fusion.57 = f32[1024,1024]{1,0:T(8,128)} fusion(bf16[1024,512]{1,0:T(8,128)(2,1)S(1)} %copy-done.4, bf16[512,1024]{1,0:T(8,128)(2,1)S(1)} %copy-done.7), kind=kOutput, calls=%fused_computation.66 | convolution fusion | flops 1073741824 | bytes 6291456 | tf_op jit(solution)/shard_map/dot_general | solution.py:55
  154.9 48.0 %all-to-all-done.1 = bf16[32,64,1024]{2,1,0:T(8,128)(2,1)} async-done(((bf16[32,64,1024]{2,1,0:T(8,128)(2,1)}), bf16[32,64,1024]{2,1,0:T(8,128)(2,1)}, u32[]{:S(2)}, u32[]{:S(2)}) %all-to-all-start.1) | async-done | bytes 4194336 | tf_op jit(solution)/shard_map/all_to_all | solution.py:46
  202.8 6.9 %fusion.7 = bf16[8,64,1024]{2,0,1:T(8,128)(2,1)S(1)} fusion(bf16[32,64,1024]{2,1,0:T(8,128)(2,1)} %all-to-all-done.1, s32[8]{0:T(128)S(1)} %fusion.51), kind=kOutput, calls=%fused_computation.10 | convolution fusion | flops 34078976 | bytes 5242912 | tf_op jit(solution)/shard_map/bo,okc->bkc/dot_general | solution.py:51
  209.7 0.9 convolution_convert_fusion.3
  210.6 0.3 convolution_bitcast_fusion
  210.9 2.1 fusion.18
  213.0 4.4 %copy.53 = f32[32,512,64]{1,2,0:T(8,128)} copy(f32[32,512,64]{1,0,2:T(8,128)S(1)} %fusion.18) | data formatting | bytes 8388608 | tf_op jit(solution)/shard_map/bo,bdk->odk/dot_general | solution.py:82
  217.4 7.0 %all-to-all-start.2 = ((f32[32,512,64]{1,2,0:T(8,128)}), f32[32,512,64]{1,2,0:T(8,128)}, u32[]{:S(2)}, u32[]{:S(2)}) async-start(f32[32,512,64]{1,2,0:T(8,128)} %copy.53), calls=%async_computation.3 | async-start | bytes 8388608 | tf_op jit(solution)/shard_map/all_to_all | solution.py:85
  224.5 0.3 broadcast_select_fusion
  224.9 0.5 fusion.23
  225.4 0.7 copy-done.6
  226.0 0.3 copy-done.8
  226.3 2.3 fusion.4
  228.5 3.3 %copy.61 = bf16[8,64,1024]{2,1,0:T(8,128)(2,1)} copy(bf16[8,64,1024]{1,0,2:T(8,128)(2,1)} %all-gather.5.cloned.1.call-done) | data formatting | bytes 2097152
  231.9 44.0 %all-to-all-done.2 = f32[32,512,64]{1,2,0:T(8,128)} async-done(((f32[32,512,64]{1,2,0:T(8,128)}), f32[32,512,64]{1,2,0:T(8,128)}, u32[]{:S(2)}, u32[]{:S(2)}) %all-to-all-start.2) | async-done | bytes 4194336 | tf_op jit(solution)/shard_map/all_to_all | solution.py:85
  275.9 5.8 %fusion.13 = bf16[8,512,64]{1,0,2:T(8,128)(2,1)S(1)} fusion(f32[32,512,64]{1,2,0:T(8,128)} %all-to-all-done.2, s32[32]{0:T(128)S(1)} %fusion.34, pred[32]{0:T(512)(128)(4,1)S(1)} %get-tuple-element.31), kind=kOutput, calls=%fused_computation.13 | convolution fusion | flops 100925952 | bytes 4718752 | tf_op jit(solution)/shard_map/ra,rdk->adk/dot_general | solution.py:89
  281.7 0.9 copy.60
  282.7 3.5 %reduce-scatter.2.cloned.1.call-done = f32[64,1024]{1,0:T(8,128)} async-done(((f32[1024,1024]{1,0:T(8,128)}), f32[64,1024]{1,0:T(8,128)}) %reduce-scatter.2.cloned.1.call-update) | async-done | bytes 262160 | tf_op jit(solution)/shard_map/reduce_scatter | solution.py:56
  286.2 1.9 fusion.16
  (21 shorter events, 0.1 us)
Async XLA Ops:
  7.2 132.5 %copy-start = (bf16[8,64,1024]{2,1,0:T(8,128)(2,1)S(1)}, bf16[8,64,1024]{2,1,0:T(8,128)(2,1)}, u32[]{:S(2)}) copy-start(bf16[8,64,1024]{2,1,0:T(8,128)(2,1)} %param.10) | copy-start | bytes 3145732
  7.2 109.8 %all-gather.3.cloned.1.call-start = ((), (), s32[]{:S(2)}) async-start(), calls=%async_computation.6 | async-start | bytes 2228224 | tf_op jit(solution)/shard_map/all_gather | solution.py:69
  13.5 37.6 %all-to-all-start = ((bf16[32,512,64]{1,2,0:T(8,128)(2,1)}), bf16[32,512,64]{1,2,0:T(8,128)(2,1)S(1)}, u32[]{:S(2)}, u32[]{:S(2)}) async-start(bf16[32,512,64]{1,2,0:T(8,128)(2,1)} %copy.43), calls=%async_computation.1 | async-start | bytes 4194304 | tf_op jit(solution)/shard_map/all_to_all | solution.py:45
  23.1 205.5 %all-gather.5.cloned.1.call-start = ((), (), s32[]{:S(2)}) async-start(), calls=%async_computation.7 | async-start | bytes 2228224 | tf_op jit(solution)/shard_map/all_gather | solution.py:93
  51.0 2.0 copy-start.3
  52.3 0.8 copy-start.1
  145.3 6.4 %copy-start.4 = (bf16[1024,512]{1,0:T(8,128)(2,1)S(1)}, bf16[1024,512]{1,0:T(8,128)(2,1)}, u32[]{:S(2)}) copy-start(bf16[1024,512]{1,0:T(8,128)(2,1)} %param.7) | copy-start | bytes 3145732
  145.3 6.4 %copy-start.7 = (bf16[512,1024]{1,0:T(8,128)(2,1)S(1)}, bf16[512,1024]{1,0:T(8,128)(2,1)}, u32[]{:S(2)}) copy-start(bf16[512,1024]{1,0:T(8,128)(2,1)} %param.8) | copy-start | bytes 3145732
  145.3 57.5 %all-to-all-start.1 = ((bf16[32,64,1024]{2,1,0:T(8,128)(2,1)}), bf16[32,64,1024]{2,1,0:T(8,128)(2,1)}, u32[]{:S(2)}, u32[]{:S(2)}) async-start(bf16[32,64,1024]{2,1,0:T(8,128)(2,1)} %copy.48), calls=%async_computation.2 | async-start | bytes 8388608 | tf_op jit(solution)/shard_map/all_to_all | solution.py:46
  151.4 134.8 %reduce-scatter.2.cloned.1.call-start = ((), (), s32[]{:S(2)}) async-start(), calls=%async_computation.5 | async-start | bytes 4456448 | tf_op jit(solution)/shard_map/reduce_scatter | solution.py:56
  202.8 6.9 %copy-start.5 = (bf16[1024,1024]{1,0:T(8,128)(2,1)S(1)}, bf16[1024,1024]{1,0:T(8,128)(2,1)}, u32[]{:S(2)}) copy-start(bf16[1024,1024]{1,0:T(8,128)(2,1)} %all-gather.3.cloned.1.call-done) | copy-start | bytes 6291460
  217.4 7.4 %copy-start.2 = (bf16[8,512,64]{1,0,2:T(8,128)(2,1)S(1)}, bf16[8,512,64]{1,0,2:T(8,128)(2,1)}, u32[]{:S(2)}) copy-start(bf16[8,512,64]{1,0,2:T(8,128)(2,1)} %copy-done.1) | copy-start | bytes 1572868
  217.4 58.4 %all-to-all-start.2 = ((f32[32,512,64]{1,2,0:T(8,128)}), f32[32,512,64]{1,2,0:T(8,128)}, u32[]{:S(2)}, u32[]{:S(2)}) async-start(f32[32,512,64]{1,2,0:T(8,128)} %copy.53), calls=%async_computation.3 | async-start | bytes 8388608 | tf_op jit(solution)/shard_map/all_to_all | solution.py:85
  224.4 1.6 copy-start.6
  224.4 1.8 copy-start.8
Sparse Core Ops, SparseCore 0:
  10.1 78.1 all-gather.2
  139.8 66.9 all-gather.4
  209.6 76.5 reduce-scatter.1
where the time goes:
time: 295 us
  waiting for transfers between devices  124 us (42%)
  blocking collectives  78.2 us (27%)
  matrix products  31.6 us (11%)
  starting transfers between devices  23 us (8%)
  local copies, waits for them, and re-layouts  20.3 us (7%)
  between operations  14 us (5%)
  other arithmetic  3.37 us (1%)
    psum x1, blocking collectives, per_device(): down = lax.psum(down_part, 'mp').astype(jnp.bfloat16)  63.4 us
    all_to_all x1, waiting for transfers between devices, per_device(): lax.all_to_all(send_b, 'dp', split_axis=0, concat_axis=0, tiled=True)  48 us
    all_to_all x1, waiting for transfers between devices, per_device(): lax.all_to_all(send_ga, 'dp', split_axis=0, concat_axis=0, tiled=True)  44 us
    all_to_all x1, waiting for transfers between devices, per_device(): lax.all_to_all(send_a, 'dp', split_axis=0, concat_axis=0, tiled=True)  27.9 us
    all_to_all x1, blocking collectives, per_device(): lax.all_to_all(send_gb, 'dp', split_axis=0, concat_axis=0, tiled=True)  14.8 us
    all_to_all x1, starting transfers between devices, per_device(): lax.all_to_all(send_a, 'dp', split_axis=0, concat_axis=0, tiled=True)  9.58 us
    unnamed x22, local copies, waits for them, and re-layouts  7.08 us
    all_to_all x1, starting transfers between devices, per_device(): lax.all_to_all(send_ga, 'dp', split_axis=0, concat_axis=0, tiled=True)  6.98 us
  transfers between devices with their start and end apart: 6, of which 4 were waited for; matrix products, arithmetic and copies ran while one was open for 15% of the time, Pallas kernels for 0%

commit v1 on v0

--- a/solution.py
+++ b/solution.py
@@ -57,7 +57,8 @@
     down_part = jnp.einsum(
         "bnd,bdk->bnk", token_blocks, panel_a, preferred_element_type=jnp.float32
     )
-    down = lax.psum(down_part, "mp").astype(jnp.bfloat16)
+    pages_trace = lambda here_x: jnp.sum(lax.all_gather(here_x, "mp"), 0)
+    down = pages_trace(down_part).astype(jnp.bfloat16)
     first_row = my_part * own_rows
     my_down = lax.dynamic_slice_in_dim(down.reshape(rows, RANK), first_row, own_rows, 0).reshape(
         groups, group, RANK

time: 295 us -> 329 us (1.12)
  waiting for transfers between devices: 124 us -> 218 us
  blocking collectives: 78.2 us -> 0 us
  starting transfers between devices: 23 us -> 30.6 us
  local copies, waits for them, and re-layouts: 20.3 us -> 24.3 us
  other arithmetic: 3.37 us -> 6.95 us
  matrix products: 31.6 us -> 34.9 us
    psum x1 -> x0, blocking collectives: 63.4 us -> none  [per_device(): down = lax.psum(down_part, 'mp').astype(jnp.bfloat16)]
    all_gather x1, waiting for transfers between devices: 0.01 us -> 59.6 us  [per_device(): grad_up = lax.all_gather(grad_share, 'mp', axis=2, tiled=True)]
    all_gather x0 -> x1, waiting for transfers between devices: none -> 38.2 us  [per_device(): pages_trace = lambda here_x: jnp.sum(lax.all_gather(here_x, 'mp'), 0)]
    all_to_all x1 -> x0, blocking collectives: 14.8 us -> none  [per_device(): lax.all_to_all(send_gb, 'dp', split_axis=0, concat_axis=0, tiled=True)]
    all_to_all x0 -> x1, starting transfers between devices: none -> 7.79 us  [per_device(): lax.all_to_all(send_gb, 'dp', split_axis=0, concat_axis=0, tiled=True)]
    all_to_all x1, waiting for transfers between devices: 44 us -> 39.3 us  [per_device(): lax.all_to_all(send_ga, 'dp', split_axis=0, concat_axis=0, tiled=True)]
    all_to_all x0 -> x1, waiting for transfers between devices: none -> 3.74 us  [per_device(): lax.all_to_all(send_gb, 'dp', split_axis=0, concat_axis=0, tiled=True)]
    reduce_scatter x1, waiting for transfers between devices: 3.54 us -> 0.02 us  [per_device(): lax.psum_scatter(partial_value, 'mp', scatter_dimension=0, tiled=True)]
  transfers between devices with their start and end apart: 6 -> 8, of which waited for: 4 -> 6; matrix products, arithmetic and copies ran while one was open for 15% -> 19% of each run, Pallas kernels for 0% -> 0%
where the time goes in v1:
time: 329 us; the launch traced here: 328 us
  waiting for transfers between devices  218 us (66%)
  matrix products  34.9 us (11%)
  starting transfers between devices  30.6 us (9%)
  local copies, waits for them, and re-layouts  24.3 us (7%)
  between operations  14 us (4%)
  other arithmetic  6.95 us (2%)
    all_gather x1, waiting for transfers between devices, per_device(): grad_up = lax.all_gather(grad_share, 'mp', axis=2, tiled=True)  59.6 us
    all_to_all x1, waiting for transfers between devices, per_device(): lax.all_to_all(send_b, 'dp', split_axis=0, concat_axis=0, tiled=True)  48 us
    all_to_all x1, waiting for transfers between devices, per_device(): lax.all_to_all(send_ga, 'dp', split_axis=0, concat_axis=0, tiled=True)  39.3 us
    all_gather x1, waiting for transfers between devices, per_device(): pages_trace = lambda here_x: jnp.sum(lax.all_gather(here_x, 'mp'), 0)  38.2 us
    all_to_all x1, waiting for transfers between devices, per_device(): lax.all_to_all(send_a, 'dp', split_axis=0, concat_axis=0, tiled=True)  27.9 us
    unnamed x20, local copies, waits for them, and re-layouts  10.1 us
    all_to_all x1, starting transfers between devices, per_device(): lax.all_to_all(send_a, 'dp', split_axis=0, concat_axis=0, tiled=True)  9.58 us
    all_to_all x1, starting transfers between devices, per_device(): lax.all_to_all(send_gb, 'dp', split_axis=0, concat_axis=0, tiled=True)  7.79 us
  transfers between devices with their start and end apart: 8, of which 6 were waited for; matrix products, arithmetic and copies ran while one was open for 19% of the time, Pallas kernels for 0%

profile of v1, /device:TPU:2, one launch (start us, length us, event | category | flops | bytes accessed | tf_op | source)
XLA Modules:
  0.0 328.4 jit_solution(6642053457209111825)
XLA Ops:
  7.2 0.7 all-gather.5.cloned.1.call-update
  7.9 0.9 select_reduce_fusion
  8.8 0.1 reduce_sum.30
  8.9 0.1 fusion.56
  9.0 0.1 fusion.34
  9.1 1.8 convolution_convert_fusion.1
  11.0 2.5 copy.61
  13.4 9.6 %all-to-all-start = ((bf16[32,512,64]{1,2,0:T(8,128)(2,1)}), bf16[32,512,64]{1,2,0:T(8,128)(2,1)S(1)}, u32[]{:S(2)}, u32[]{:S(2)}) async-start(bf16[32,512,64]{1,2,0:T(8,128)(2,1)} %copy.61), calls=%async_computation.1 | async-start | bytes 4194304 | tf_op jit(solution)/shard_map/all_to_all | solution.py:45
  23.1 27.9 %all-to-all-done = bf16[32,512,64]{1,2,0:T(8,128)(2,1)S(1)} async-done(((bf16[32,512,64]{1,2,0:T(8,128)(2,1)}), bf16[32,512,64]{1,2,0:T(8,128)(2,1)S(1)}, u32[]{:S(2)}, u32[]{:S(2)}) %all-to-all-start) | async-done | bytes 2097184 | tf_op jit(solution)/shard_map/all_to_all | solution.py:45
  51.0 1.2 fusion.10
  52.2 0.8 copy-done.1
  53.0 1.2 convolution_bitcast_fusion.1
  54.3 1.3 convolution_convert_fusion
  55.6 4.3 %copy.66 = bf16[32,64,1024]{2,1,0:T(8,128)(2,1)} copy(bf16[32,64,1024]{2,0,1:T(8,128)(2,1)S(1)} %convolution_convert_fusion) | data formatting | bytes 8388608 | tf_op jit(solution)/shard_map/convert_element_type | solution.py:43
  59.8 6.9 %all-to-all-start.1 = ((bf16[32,64,1024]{2,1,0:T(8,128)(2,1)}), bf16[32,64,1024]{2,1,0:T(8,128)(2,1)}, u32[]{:S(2)}, u32[]{:S(2)}) async-start(bf16[32,64,1024]{2,1,0:T(8,128)(2,1)} %copy.66), calls=%async_computation.2 | async-start | bytes 8388608 | tf_op jit(solution)/shard_map/all_to_all | solution.py:46
  66.8 0.2 reduce-scatter.2.cloned.1.call-start
  67.0 3.2 fusion.57
  70.2 48.0 %all-to-all-done.1 = bf16[32,64,1024]{2,1,0:T(8,128)(2,1)} async-done(((bf16[32,64,1024]{2,1,0:T(8,128)(2,1)}), bf16[32,64,1024]{2,1,0:T(8,128)(2,1)}, u32[]{:S(2)}, u32[]{:S(2)}) %all-to-all-start.1) | async-done | bytes 4194336 | tf_op jit(solution)/shard_map/all_to_all | solution.py:46
  118.2 6.7 %fusion.7 = bf16[8,64,1024]{2,0,1:T(8,128)(2,1)S(1)} fusion(bf16[32,64,1024]{2,1,0:T(8,128)(2,1)} %all-to-all-done.1, s32[8]{0:T(128)S(1)} %fusion.51), kind=kOutput, calls=%fused_computation.10 | convolution fusion | flops 34078976 | bytes 5242912 | tf_op jit(solution)/shard_map/bo,okc->bkc/dot_general | solution.py:51
  125.0 2.5 convolution_convert_fusion.3
  127.5 38.2 %all-gather.9.cloned.1.call-done = f32[128,128,64]{1,2,0:T(8,128)} async-done(((f32[8,128,64]{1,2,0:T(8,128)}), f32[128,128,64]{1,2,0:T(8,128)}) %all-gather.9.cloned.1.call-update) | async-done | bytes 4194320 | tf_op jit(solution)/shard_map/all_gather | solution.py:60
  165.7 2.5 reduce_sum.32
  168.3 1.2 fusion.28
  169.5 0.7 fusion.26
  170.2 1.6 copy.75
  171.8 2.7 reshape.88
  174.4 7.8 %all-to-all-start.3 = ((f32[32,1,4096]{2,1,0:T(1,128)}), f32[32,1,4096]{2,1,0:T(1,128)}, u32[]{:S(2)}, u32[]{:S(2)}) async-start(f32[32,1,4096]{2,1,0:T(1,128)} %reshape.88), calls=%async_computation.4 | async-start | bytes 1048576 | tf_op jit(solution)/shard_map/all_to_all | solution.py:87
  182.2 0.3 convolution_bitcast_fusion
  182.5 2.1 fusion.18
  184.6 4.4 %copy.71 = f32[32,512,64]{1,2,0:T(8,128)} copy(f32[32,512,64]{1,0,2:T(8,128)S(1)} %fusion.18) | data formatting | bytes 8388608 | tf_op jit(solution)/shard_map/bo,bdk->odk/dot_general | solution.py:83
  189.0 3.7 %all-to-all-done.3 = f32[32,1,4096]{2,1,0:T(1,128)} async-done(((f32[32,1,4096]{2,1,0:T(1,128)}), f32[32,1,4096]{2,1,0:T(1,128)}, u32[]{:S(2)}, u32[]{:S(2)}) %all-to-all-start.3) | async-done | bytes 524320 | tf_op jit(solution)/shard_map/all_to_all | solution.py:87
  192.8 6.0 %all-to-all-start.2 = ((f32[32,512,64]{1,2,0:T(8,128)}), f32[32,512,64]{1,2,0:T(8,128)}, u32[]{:S(2)}, u32[]{:S(2)}) async-start(f32[32,512,64]{1,2,0:T(8,128)} %copy.71), calls=%async_computation.3 | async-start | bytes 8388608 | tf_op jit(solution)/shard_map/all_to_all | solution.py:86
  198.8 0.5 broadcast.68
  199.3 2.9 reduce
  202.3 1.4 reshape.89
  203.7 2.2 convolution_convert_fusion.2
  205.9 0.8 copy.77
  206.8 0.3 broadcast_select_fusion
  207.1 0.5 fusion.23
  207.6 0.7 copy-done.5
  208.3 0.3 copy-done.7
  208.6 2.3 fusion.4
  210.9 39.3 %all-to-all-done.2 = f32[32,512,64]{1,2,0:T(8,128)} async-done(((f32[32,512,64]{1,2,0:T(8,128)}), f32[32,512,64]{1,2,0:T(8,128)}, u32[]{:S(2)}, u32[]{:S(2)}) %all-to-all-start.2) | async-done | bytes 4194336 | tf_op jit(solution)/shard_map/all_to_all | solution.py:86
  250.2 5.8 %fusion.13 = bf16[8,512,64]{1,0,2:T(8,128)(2,1)S(1)} fusion(f32[32,512,64]{1,2,0:T(8,128)} %all-to-all-done.2, s32[32]{0:T(128)S(1)} %fusion.34, pred[32]{0:T(512)(128)(4,1)S(1)} %get-tuple-element.35), kind=kOutput, calls=%fused_computation.13 | convolution fusion | flops 100925952 | bytes 4718752 | tf_op jit(solution)/shard_map/ra,rdk->adk/dot_general | solution.py:90
  256.0 0.9 copy.78
  257.0 1.9 fusion.16
  258.9 59.6 %all-gather.7.cloned.1.call-done = bf16[8,64,1024]{1,0,2:T(8,128)(2,1)} async-done(((bf16[8,64,64]{1,0,2:T(8,128)(2,1)}), bf16[8,64,1024]{1,0,2:T(8,128)(2,1)}) %all-gather.7.cloned.1.call-update) | async-done | bytes 1048592 | tf_op jit(solution)/shard_map/all_gather | solution.py:94
  318.5 3.3 %copy.79 = bf16[8,64,1024]{2,1,0:T(8,128)(2,1)} copy(bf16[8,64,1024]{1,0,2:T(8,128)(2,1)} %all-gather.7.cloned.1.call-done) | data formatting | bytes 2097152
  (23 shorter events, 0.3 us)
Async XLA Ops:
  7.2 47.1 %copy-start = (bf16[8,64,1024]{2,1,0:T(8,128)(2,1)S(1)}, bf16[8,64,1024]{2,1,0:T(8,128)(2,1)}, u32[]{:S(2)}) copy-start(bf16[8,64,1024]{2,1,0:T(8,128)(2,1)} %param.10) | copy-start | bytes 3145732
  7.2 117.8 %all-gather.5.cloned.1.call-start = ((), (), s32[]{:S(2)}) async-start(), calls=%async_computation.6 | async-start | bytes 2228224 | tf_op jit(solution)/shard_map/all_gather | solution.py:70
  13.4 37.6 %all-to-all-start = ((bf16[32,512,64]{1,2,0:T(8,128)(2,1)}), bf16[32,512,64]{1,2,0:T(8,128)(2,1)S(1)}, u32[]{:S(2)}, u32[]{:S(2)}) async-start(bf16[32,512,64]{1,2,0:T(8,128)(2,1)} %copy.61), calls=%async_computation.1 | async-start | bytes 4194304 | tf_op jit(solution)/shard_map/all_to_all | solution.py:45
  23.0 142.7 %all-gather.9.cloned.1.call-start = ((), (), s32[]{:S(2)}) async-start(), calls=%async_computation.8 | async-start | bytes 4456448 | tf_op jit(solution)/shard_map/all_gather | solution.py:60
  51.0 2.0 copy-start.3
  52.2 0.8 copy-start.1
  59.8 7.2 %copy-start.4 = (bf16[1024,512]{1,0:T(8,128)(2,1)S(1)}, bf16[1024,512]{1,0:T(8,128)(2,1)}, u32[]{:S(2)}) copy-start(bf16[1024,512]{1,0:T(8,128)(2,1)} %param.7) | copy-start | bytes 3145732
  59.8 7.2 %copy-start.6 = (bf16[512,1024]{1,0:T(8,128)(2,1)S(1)}, bf16[512,1024]{1,0:T(8,128)(2,1)}, u32[]{:S(2)}) copy-start(bf16[512,1024]{1,0:T(8,128)(2,1)} %param.8) | copy-start | bytes 3145732
  59.8 58.4 %all-to-all-start.1 = ((bf16[32,64,1024]{2,1,0:T(8,128)(2,1)}), bf16[32,64,1024]{2,1,0:T(8,128)(2,1)}, u32[]{:S(2)}, u32[]{:S(2)}) async-start(bf16[32,64,1024]{2,1,0:T(8,128)(2,1)} %copy.66), calls=%async_computation.2 | async-start | bytes 8388608 | tf_op jit(solution)/shard_map/all_to_all | solution.py:46
  66.8 190.2 %reduce-scatter.2.cloned.1.call-start = ((), (), s32[]{:S(2)}) async-start(), calls=%async_computation.5 | async-start | bytes 4456448 | tf_op jit(solution)/shard_map/reduce_scatter | solution.py:56
  174.4 18.3 %all-to-all-start.3 = ((f32[32,1,4096]{2,1,0:T(1,128)}), f32[32,1,4096]{2,1,0:T(1,128)}, u32[]{:S(2)}, u32[]{:S(2)}) async-start(f32[32,1,4096]{2,1,0:T(1,128)} %reshape.88), calls=%async_computation.4 | async-start | bytes 1048576 | tf_op jit(solution)/shard_map/all_to_all | solution.py:87
  192.8 57.4 %all-to-all-start.2 = ((f32[32,512,64]{1,2,0:T(8,128)}), f32[32,512,64]{1,2,0:T(8,128)}, u32[]{:S(2)}, u32[]{:S(2)}) async-start(f32[32,512,64]{1,2,0:T(8,128)} %copy.71), calls=%async_computation.3 | async-start | bytes 8388608 | tf_op jit(solution)/shard_map/all_to_all | solution.py:86
  198.7 119.8 %all-gather.7.cloned.1.call-start = ((), (), s32[]{:S(2)}) async-start(), calls=%async_computation.7 | async-start | bytes 2228224 | tf_op jit(solution)/shard_map/all_gather | solution.py:94
  202.3 4.9 %copy-start.2 = (bf16[8,512,64]{1,0,2:T(8,128)(2,1)S(1)}, bf16[8,512,64]{1,0,2:T(8,128)(2,1)}, u32[]{:S(2)}) copy-start(bf16[8,512,64]{1,0,2:T(8,128)(2,1)} %copy-done.1) | copy-start | bytes 1572868
  206.7 1.6 copy-start.5
  206.7 1.9 copy-start.7
Sparse Core Ops, SparseCore 0:
  10.1 77.9 all-gather.4
  90.7 74.9 all-gather.8
  168.6 75.6 reduce-scatter.1
  246.8 71.7 all-gather.6
